TPU v7x, 256 devices: a whole 4x4x8 slice. The times are simulated.
256 devices in a mesh: frow: 16 (over z, x_lo), fcol: 16 (over y, x_hi, core).
Axes of the slice: x: 4 (x_hi: 2, x_lo: 2; x = x_hi * 2 + x_lo), y: 4, z: 8, core: 2. Of those that a mesh axis runs over, the one named last changes fastest.
Arguments:
- facets: float32 [2, 2048, 16384], P(None, 'frow', 'fcol'), may hold values from -6 to 6
- column_start: int32 [1], replicated, may hold values from 0 to 16383
- subgrid_start: int32 [16], replicated, may hold values from 0 to 2047
- vis_count: int32 [16], P('frow'), may hold values from 1 to 64
- vis_row: int32 [16, 64], P('frow'), may hold values from 0 to 511
- vis_weight: float32 [16, 64, 512], P('frow', None, 'fcol'), may hold values from -1 to 1
Outputs:
- corrected: float32 [16, 512, 2, 512], P('frow', 'fcol')
- facet_update: float32 [2, 2048, 16384], P(None, 'frow', 'fcol')
All inputs are finite; a program needn't handle non-finite values.
Results may differ from a plain program's by a relative error of at most 0.0003.
Values sent between devices are 32-bit elements; how exact they have to be, the bound alone decides.
A program may use at most 64 MiB of HBM per device.

v0:
```python
import math
import jax
import jax.numpy as jnp
from jax import lax
from jax.sharding import PartitionSpec as P

SG = 512
MAXB = 64
HIGH = lax.Precision.HIGHEST


def table(first, count, anchor, length, modulus):
    freqs = (first + jnp.arange(count, dtype=jnp.int32)) % modulus
    coords = anchor + jnp.arange(length, dtype=jnp.int32)
    phase = freqs[:, None] * coords[None, :] % modulus
    angle = phase.astype(jnp.float32) * jnp.float32(2.0 * math.pi / modulus)
    scale = jnp.float32(1.0 / math.sqrt(modulus))
    return (jnp.cos(angle) * scale, jnp.sin(angle) * scale)


def table_batch(firsts, anchors, count, length, modulus):
    freqs = (firsts[..., None] + jnp.arange(count, dtype=jnp.int32)) % modulus
    coords = anchors[..., None] + jnp.arange(length, dtype=jnp.int32)
    phase = freqs[..., :, None] * coords[..., None, :] % modulus
    angle = phase.astype(jnp.float32) * jnp.float32(2.0 * math.pi / modulus)
    scale = jnp.float32(1.0 / math.sqrt(modulus))
    return (jnp.cos(angle) * scale, jnp.sin(angle) * scale)


def contract(form, left, right):
    return jnp.einsum(form, left, right, precision=HIGH)


def per_device(facets, column_start, subgrid_start, vis_count, vis_row, vis_weight):
    row_index = lax.axis_index("frow")
    col_index = lax.axis_index("fcol")
    row_devices = lax.axis_size("frow")
    col_devices = lax.axis_size("fcol")
    height, width = (facets.shape[1], facets.shape[2])
    rows_total = height * row_devices
    cols_total = width * col_devices
    sub_owned = vis_count.shape[0]
    col_local = SG // col_devices
    real_part, imag_part = (facets[0], facets[1])
    col_cos, col_sin = table(
        column_start[0], col_local * lax.axis_size("fcol"), col_index * width, width, cols_total
    )
    strip_re = contract("qy,xy->qx", col_cos, real_part) + contract("qy,xy->qx", col_sin, imag_part)
    strip_im = contract("qy,xy->qx", col_cos, imag_part) - contract("qy,xy->qx", col_sin, real_part)
    strip = lax.psum_scatter(
        jnp.stack([strip_re, strip_im], 1), "fcol", scatter_dimension=0, tiled=True
    )
    anchors = jnp.zeros((sub_owned * lax.axis_size("frow"),), jnp.int32) + row_index * height
    row_cos, row_sin = table_batch(subgrid_start, anchors, SG, height, rows_total)
    sub_re = contract("qx,spx->sqp", strip[:, 0], row_cos) + contract(
        "qx,spx->sqp", strip[:, 1], row_sin
    )
    sub_im = contract("qx,spx->sqp", strip[:, 1], row_cos) - contract(
        "qx,spx->sqp", strip[:, 0], row_sin
    )
    subs = lax.psum_scatter(jnp.stack([sub_re, sub_im], 2), "frow", scatter_dimension=0, tiled=True)
    live = (jnp.arange(MAXB, dtype=jnp.int32)[None, :] < vis_count[:, None]).astype(jnp.float32)
    onehot = (vis_row[:, :, None] == jnp.arange(SG, dtype=jnp.int32)[None, None, :]).astype(
        jnp.float32
    )
    gain = 1.0 + contract("sbq,sbp->sqp", vis_weight * live[:, :, None], onehot)
    corrected = subs * gain[:, :, None, :]
    piece = lax.all_gather(corrected, "frow", axis=0, tiled=True)
    count = piece.shape[0]
    anchors = jnp.zeros((count,), jnp.int32) + row_index * height
    row_cos, row_sin = table_batch(subgrid_start, anchors, SG, height, rows_total)
    back_re = contract("mqp,mpx->qx", piece[:, :, 0], row_cos) - contract(
        "mqp,mpx->qx", piece[:, :, 1], row_sin
    )
    back_im = contract("mqp,mpx->qx", piece[:, :, 1], row_cos) + contract(
        "mqp,mpx->qx", piece[:, :, 0], row_sin
    )
    back = jnp.stack([back_re, back_im], 1)
    piece = lax.all_gather(back, "fcol", axis=0, tiled=True)
    col_cos, col_sin = table(column_start[0], piece.shape[0], col_index * width, width, cols_total)
    image_re = contract("qx,qy->xy", piece[:, 0], col_cos) - contract(
        "qx,qy->xy", piece[:, 1], col_sin
    )
    image_im = contract("qx,qy->xy", piece[:, 1], col_cos) + contract(
        "qx,qy->xy", piece[:, 0], col_sin
    )
    facet_update = jnp.stack([image_re, image_im])
    return (corrected, facet_update)


def solution(mesh):
    return jax.shard_map(
        per_device,
        mesh=mesh,
        in_specs=(
            P(None, "frow", "fcol"),
            P(),
            P(),
            P("frow"),
            P("frow", None),
            P("frow", None, "fcol"),
        ),
        out_specs=(P("frow", "fcol", None, None), P(None, "frow", "fcol")),
        check_vma=False,
    )
```

profile of v0, /device:TPU:1, one launch (start us, length us, event | category | flops | bytes accessed | tf_op | source)
XLA Modules:
  0.0 582.7 jit_solution(18072297512777448642)
XLA Ops:
  7.2 0.0 reduce-scatter.5.cloned.1.call-start
  7.9 0.0 copy-start.4
  7.9 10.5 %fusion.33 = f32[512,128]{1,0:T(8,128)S(1)} fusion(s32[1024]{0:T(1024)S(1)} %iota_add_fusion, s32[512]{0:T(512)S(1)} %add_select_fusion.3, f32[2,128,1024]{2,1,0:T(8,128)} %param.6), kind=kOutput, calls=%fused_computation.40 | convolution fusion | flops 813170688 | bytes 792576 | tf_op jit(solution)/shard_map/qy,xy->qx/dot_general | solution.py:31
  18.4 0.0 copy-done.4
  18.4 9.6 %fusion.32 = f32[512,128]{1,0:T(8,128)S(1)} fusion(s32[1024]{0:T(1024)S(1)} %iota_add_fusion, s32[512]{0:T(512)S(1)} %add_select_fusion.3, f32[2,128,1024]{2,1,0:T(8,128)S(1)} %copy-done.4), kind=kOutput, calls=%fused_computation.39 | convolution fusion | flops 813170688 | bytes 792576 | tf_op jit(solution)/shard_map/qy,xy->qx/dot_general | solution.py:31
  28.0 9.9 %fusion.47 = f32[512,1,128]{2,0,1:T(8,128)S(1)} fusion(f32[512,128]{1,0:T(8,128)S(1)} %fusion.33, s32[1024]{0:T(1024)S(1)} %iota_add_fusion, s32[512]{0:T(512)S(1)} %add_select_fusion.3, f32[2,128,1024]{2,1,0:T(8,128)S(1)} %copy-done.4), kind=kOutput, calls=%fused_computation.54 | convolution fusion | flops 813236224 | bytes 1054720 | tf_op jit(solution)/shard_map/qy,xy->qx/dot_general | solution.py:31
  37.9 0.0 copy-start.1
  37.9 9.6 %fusion.49 = f32[512,1,128]{2,0,1:T(8,128)S(1)} fusion(f32[512,128]{1,0:T(8,128)S(1)} %fusion.32, s32[1024]{0:T(1024)S(1)} %iota_add_fusion, s32[512]{0:T(512)S(1)} %add_select_fusion.3, f32[2,128,1024]{2,1,0:T(8,128)S(1)} %copy-done.4), kind=kOutput, calls=%fused_computation.56 | convolution fusion | flops 813236224 | bytes 1054720 | tf_op jit(solution)/shard_map/qy,xy->qx/dot_general | solution.py:31
  47.5 0.8 pad_maximum_fusion.2
  48.3 0.0 reduce-scatter.5.cloned.1.call-update
  48.3 0.0 all-reduce.3.cloned.1.call-start
  48.4 0.0 copy-done.1
  48.4 0.1 add_select_fusion.2
  48.5 75.3 %reduce-scatter.5.cloned.1.call-done = f32[32,2,128]{2,0,1:T(8,128)} async-done(((f32[512,2,128]{2,0,1:T(8,128)}), f32[32,2,128]{2,0,1:T(8,128)}) %reduce-scatter.5.cloned.1.call-update) | async-done | bytes 32784 | tf_op jit(solution)/shard_map/reduce_scatter | solution.py:50
  123.8 0.0 copy-start.5
  123.8 21.4 %fusion.6 = f32[16,512,32]{1,2,0:T(8,128)S(1)} fusion(s32[128]{0:T(128)S(1)} %iota_add_fusion.1, s32[16,512]{1,0:T(8,128)S(1)} %add_select_fusion.2, f32[32,2,128]{2,0,1:T(8,128)} %reduce-scatter.5.cloned.1.call-done), kind=kOutput, calls=%fused_computation.18 | convolution fusion | flops 418381824 | bytes 1098240 | tf_op jit(solution)/shard_map/qx,spx->sqp/dot_general | solution.py:31
  145.1 0.0 copy-done.5
  145.1 20.6 %fusion.5 = f32[16,512,32]{1,2,0:T(8,128)S(1)} fusion(s32[128]{0:T(128)S(1)} %iota_add_fusion.1, s32[16,512]{1,0:T(8,128)S(1)} %add_select_fusion.2, f32[32,2,128]{2,0,1:T(8,128)S(1)} %copy-done.5), kind=kOutput, calls=%fused_computation.17 | convolution fusion | flops 418381824 | bytes 1098240 | tf_op jit(solution)/shard_map/qx,spx->sqp/dot_general | solution.py:31
  165.7 20.8 %fusion.39 = f32[16,32,1,512]{3,1,0,2:T(8,128)S(1)} fusion(f32[16,512,32]{1,2,0:T(8,128)S(1)} %fusion.6, s32[128]{0:T(128)S(1)} %iota_add_fusion.1, s32[16,512]{1,0:T(8,128)S(1)} %add_select_fusion.2, f32[32,2,128]{2,0,1:T(8,128)S(1)} %copy-done.5), kind=kOutput, calls=%fused_computation.46 | convolution fusion | flops 418643968 | bytes 2146816 | tf_op jit(solution)/shard_map/qx,spx->sqp/dot_general | solution.py:31
  186.5 20.8 %fusion.41 = f32[16,32,1,512]{3,1,0,2:T(8,128)S(1)} fusion(f32[16,512,32]{1,2,0:T(8,128)S(1)} %fusion.5, s32[128]{0:T(128)S(1)} %iota_add_fusion.1, s32[16,512]{1,0:T(8,128)S(1)} %add_select_fusion.2, f32[32,2,128]{2,0,1:T(8,128)S(1)} %copy-done.5), kind=kOutput, calls=%fused_computation.48 | convolution fusion | flops 418643968 | bytes 2146816 | tf_op jit(solution)/shard_map/qx,spx->sqp/dot_general | solution.py:31
  207.3 1.5 pad_maximum_fusion
  208.8 0.0 copy-start.6
  208.8 0.0 copy-start
  208.8 0.0 copy-start.2
  208.8 0.0 all-reduce.3.cloned.1.call-update
  208.9 0.3 all-gather.2.cloned.1.call-start
  209.8 0.0 copy-done.6
  209.8 0.6 dynamic-slice
  210.4 0.0 copy-done
  210.4 0.0 copy-done.2
  210.4 0.2 convolution_add_fusion
  210.6 136.5 %all-reduce.3.cloned.1.call-done = f32[16,32,2,512]{3,1,0,2:T(8,128)} async-done(((f32[16,32,2,512]{3,1,0,2:T(8,128)}), f32[16,32,2,512]{3,1,0,2:T(8,128)}) %all-reduce.3.cloned.1.call-update) | async-done | bytes 2097168
  347.1 2.2 dynamic-slice_multiply_fusion
  349.3 0.0 all-gather.2.cloned.1.call-update
  349.3 1.7 copy.10
  351.0 69.5 %all-gather.2.cloned.1.call-done = f32[16,32,2,512]{3,1,0,2:T(8,128)} async-done(((f32[1,32,2,512]{3,1,0,2:T(8,128)}), f32[16,32,2,512]{3,1,0,2:T(8,128)}) %all-gather.2.cloned.1.call-update) | async-done | bytes 2097168 | tf_op jit(solution)/shard_map/all_gather | solution.py:68
  420.5 0.0 copy-start.3
  420.5 22.2 %fusion.50 = f32[32,128]{1,0:T(8,128)S(1)} fusion(s32[128]{0:T(128)S(1)} %iota_add_fusion.1, s32[16,512]{1,0:T(8,128)S(1)} %add_select_fusion.2, f32[16,32,2,512]{3,1,0,2:T(8,128)} %all-gather.2.cloned.1.call-done), kind=kOutput, calls=%fused_computation.58 | convolution fusion | flops 418381824 | bytes 1098240 | tf_op jit(solution)/shard_map/mqp,mpx->qx/dot_general | solution.py:31
  442.7 0.0 copy-done.3
  442.7 19.3 %fusion.51 = f32[32,128]{1,0:T(8,128)S(1)} fusion(s32[128]{0:T(128)S(1)} %iota_add_fusion.1, s32[16,512]{1,0:T(8,128)S(1)} %add_select_fusion.2, f32[16,32,2,512]{3,1,0,2:T(8,128)S(1)} %copy-done.3), kind=kOutput, calls=%fused_computation.59 | convolution fusion | flops 418381824 | bytes 1098240 | tf_op jit(solution)/shard_map/mqp,mpx->qx/dot_general | solution.py:31
  462.0 19.2 %fusion.57 = f32[32,1,128]{2,0,1:T(8,128)S(1)} fusion(f32[32,128]{1,0:T(8,128)S(1)} %fusion.50, s32[128]{0:T(128)S(1)} %iota_add_fusion.1, s32[16,512]{1,0:T(8,128)S(1)} %add_select_fusion.2, f32[16,32,2,512]{3,1,0,2:T(8,128)S(1)} %copy-done.3), kind=kOutput, calls=%fused_computation.65 | convolution fusion | flops 418385920 | bytes 1114624 | tf_op jit(solution)/shard_map/mqp,mpx->qx/dot_general | solution.py:31
  481.1 19.2 %fusion.55 = f32[32,1,128]{2,0,1:T(8,128)S(1)} fusion(f32[32,128]{1,0:T(8,128)S(1)} %fusion.51, s32[128]{0:T(128)S(1)} %iota_add_fusion.1, s32[16,512]{1,0:T(8,128)S(1)} %add_select_fusion.2, f32[16,32,2,512]{3,1,0,2:T(8,128)S(1)} %copy-done.3), kind=kOutput, calls=%fused_computation.63 | convolution fusion | flops 418385920 | bytes 1114624 | tf_op jit(solution)/shard_map/mqp,mpx->qx/dot_general | solution.py:31
  500.3 37.8 %all_gather.7 = f32[512,2,128]{2,0,1:T(8,128)S(1)} all-gather(f32[32,2,128]{2,0,1:T(8,128)S(1)} %pad_maximum_fusion.3), channel_id=1, replica_groups=mesh['frow'=16,'fcol'=16] {'fcol'}, dimensions={0}, use_global_device_ids=true | all-gather | bytes 557056 | tf_op jit(solution)/shard_map/all_gather | solution.py:79
  538.1 9.0 %fusion.31 = f32[128,1024]{1,0:T(8,128)S(1)} fusion(s32[1024]{0:T(1024)S(1)} %iota_add_fusion, s32[512]{0:T(512)S(1)} %add_select_fusion.3, f32[512,2,128]{2,0,1:T(8,128)S(1)} %all_gather.7), kind=kOutput, calls=%fused_computation.38 | convolution fusion | flops 813170688 | bytes 792576 | tf_op jit(solution)/shard_map/qx,qy->xy/dot_general | solution.py:31
  547.1 9.2 %fusion.30 = f32[128,1024]{1,0:T(8,128)S(1)} fusion(s32[1024]{0:T(1024)S(1)} %iota_add_fusion, s32[512]{0:T(512)S(1)} %add_select_fusion.3, f32[512,2,128]{2,0,1:T(8,128)S(1)} %all_gather.7), kind=kOutput, calls=%fused_computation.37 | convolution fusion | flops 813170688 | bytes 792576 | tf_op jit(solution)/shard_map/qx,qy->xy/dot_general | solution.py:31
  556.3 9.3 %fusion.43 = f32[1,128,1024]{2,1,0:T(8,128)S(1)} fusion(f32[128,1024]{1,0:T(8,128)S(1)} %fusion.31, s32[1024]{0:T(1024)S(1)} %iota_add_fusion, s32[512]{0:T(512)S(1)} %add_select_fusion.3, f32[512,2,128]{2,0,1:T(8,128)S(1)} %all_gather.7), kind=kOutput, calls=%fused_computation.50 | convolution fusion | flops 813301760 | bytes 1316864 | tf_op jit(solution)/shard_map/qx,qy->xy/dot_general | solution.py:31
  565.6 9.1 %fusion.45 = f32[1,128,1024]{2,1,0:T(8,128)S(1)} fusion(f32[128,1024]{1,0:T(8,128)S(1)} %fusion.30, s32[1024]{0:T(1024)S(1)} %iota_add_fusion, s32[512]{0:T(512)S(1)} %add_select_fusion.3, f32[512,2,128]{2,0,1:T(8,128)S(1)} %all_gather.7), kind=kOutput, calls=%fused_computation.52 | convolution fusion | flops 813301760 | bytes 1316864 | tf_op jit(solution)/shard_map/qx,qy->xy/dot_general | solution.py:31
  574.7 1.1 pad_maximum_fusion.1
  (5 shorter events, 0.0 us)
Async XLA Ops:
  7.2 116.6 %reduce-scatter.5.cloned.1.call-start = ((), (), s32[]{:S(2)}) async-start(), calls=%async_computation.1 | async-start | bytes 557056 | tf_op jit(solution)/shard_map/reduce_scatter | solution.py:50
  7.9 10.5 %copy-start.4 = (f32[2,128,1024]{2,1,0:T(8,128)S(1)}, f32[2,128,1024]{2,1,0:T(8,128)}, u32[]{:S(2)}) copy-start(f32[2,128,1024]{2,1,0:T(8,128)} %param.6) | copy-start | bytes 3145732
  37.9 10.5 %copy-start.1 = (s32[16]{0:T(128)S(1)}, s32[16]{0:T(128)}, u32[]{:S(2)}) copy-start(s32[16]{0:T(128)} %param.8) | copy-start | bytes 196
  48.3 298.8 %all-reduce.3.cloned.1.call-start = ((), (), s32[]{:S(2)}) async-start(), calls=%async_computation.3 | async-start | bytes 4194304
  123.8 21.4 %copy-start.5 = (f32[32,2,128]{2,0,1:T(8,128)S(1)}, f32[32,2,128]{2,0,1:T(8,128)}, u32[]{:S(2)}) copy-start(f32[32,2,128]{2,0,1:T(8,128)} %reduce-scatter.5.cloned.1.call-done) | copy-start | bytes 98308
  208.8 0.9 copy-start.6
  208.8 1.5 copy-start
  208.8 1.5 copy-start.2
  208.9 211.7 %all-gather.2.cloned.1.call-start = ((), (), s32[]{:S(2)}) async-start(), calls=%async_computation.2 | async-start | bytes 2228224 | tf_op jit(solution)/shard_map/all_gather | solution.py:68
  420.5 22.2 %copy-start.3 = (f32[16,32,2,512]{3,1,0,2:T(8,128)S(1)}, f32[16,32,2,512]{3,1,0,2:T(8,128)}, u32[]{:S(2)}) copy-start(f32[16,32,2,512]{3,1,0,2:T(8,128)} %all-gather.2.cloned.1.call-done) | copy-start | bytes 6291460
Sparse Core Ops, SparseCore 0:
  48.5 75.2 reduce-scatter.4
  209.0 138.0 all-reduce.2
  349.5 71.0 all-gather.1
where the time goes:
time: 592 us; the launch traced here: 583 us
  waiting for transfers between devices  281 us (47%)
  matrix products  240 us (41%)
  blocking collectives  37.8 us (6%)
  between operations  15.7 us (3%)
    dot_general x17, matrix products, contract(): return jnp.einsum(form, left, right, precision=HIGH)  240 us
    unnamed x4, waiting for transfers between devices  137 us
    reduce_scatter x1, waiting for transfers between devices, per_device(): lax.psum_scatter(jnp.stack([strip_re, strip_im], 1), 'fcol', scatter_dime...  75.3 us
    all_gather x1, waiting for transfers between devices, per_device(): piece = lax.all_gather(corrected, 'frow', axis=0, tiled=True)  69.5 us
    all_gather x1, blocking collectives, per_device(): piece = lax.all_gather(back, 'fcol', axis=0, tiled=True)  37.8 us
  transfers between devices with their start and end apart: 3, of which 3 were waited for; matrix products, arithmetic and copies ran while one was open for 0% of the time, Pallas kernels for 0%

commit v1 on v0

--- a/solution.py
+++ b/solution.py
@@ -65,7 +65,10 @@
     )
     gain = 1.0 + contract("sbq,sbp->sqp", vis_weight * live[:, :, None], onehot)
     corrected = subs * gain[:, :, None, :]
-    piece = lax.all_gather(corrected, "frow", axis=0, tiled=True)
+    count_2 = lax.axis_size("frow")
+    shards = jnp.stack([corrected for _ in range(count_2)])
+    shards = lax.all_to_all(shards, "frow", split_axis=0, concat_axis=0)
+    piece = jnp.concatenate(shards, axis=0)
     count = piece.shape[0]
     anchors = jnp.zeros((count,), jnp.int32) + row_index * height
     row_cos, row_sin = table_batch(subgrid_start, anchors, SG, height, rows_total)

time: 592 us -> 563 us (0.951)
  waiting for transfers between devices: 281 us -> 249 us
    all_gather x1 -> x0, waiting for transfers between devices: 69.5 us -> none  [per_device(): piece = lax.all_gather(corrected, 'frow', axis=0, tiled=True)]
    all_to_all x0 -> x1, waiting for transfers between devices: none -> 36.3 us  [per_device(): shards = lax.all_to_all(shards, 'frow', split_axis=0, concat_axis=0)]
    unnamed x4 -> x3, waiting for transfers between devices: 137 us -> 137 us
  transfers between devices with their start and end apart: 3 -> 3, of which waited for: 3 -> 3; matrix products, arithmetic and copies ran while one was open for 0% -> 1% of each run, Pallas kernels for 0% -> 0%
where the time goes in v1:
time: 563 us; the launch traced here: 554 us
  waiting for transfers between devices  249 us (44%)
  matrix products  237 us (42%)
  blocking collectives  38.3 us (7%)
  between operations  15.8 us (3%)
  other arithmetic  6.67 us (1%)
    dot_general x17, matrix products, contract(): return jnp.einsum(form, left, right, precision=HIGH)  237 us
    unnamed x3, waiting for transfers between devices  137 us
    reduce_scatter x1, waiting for transfers between devices, per_device(): lax.psum_scatter(jnp.stack([strip_re, strip_im], 1), 'fcol', scatter_dime...  75.2 us
    all_gather x1, blocking collectives, per_device(): piece = lax.all_gather(back, 'fcol', axis=0, tiled=True)  38.3 us
    all_to_all x1, waiting for transfers between devices, per_device(): shards = lax.all_to_all(shards, 'frow', split_axis=0, concat_axis=0)  36.3 us
  transfers between devices with their start and end apart: 3, of which 3 were waited for; matrix products, arithmetic and copies ran while one was open for 1% of the time, Pallas kernels for 0%

profile of v1, /device:TPU:1, one launch (start us, length us, event | category | flops | bytes accessed | tf_op | source)
XLA Modules:
  0.0 554.2 jit_solution(12539753904108720818)
XLA Ops:
  7.2 0.0 reduce-scatter.5.cloned.1.call-start
  7.9 0.0 copy-start.3
  7.9 10.5 %fusion.32 = f32[512,128]{1,0:T(8,128)S(1)} fusion(s32[1024]{0:T(1024)S(1)} %iota_add_fusion, s32[512]{0:T(512)S(1)} %add_select_fusion.3, f32[2,128,1024]{2,1,0:T(8,128)} %param.6), kind=kOutput, calls=%fused_computation.40 | convolution fusion | flops 813170688 | bytes 792576 | tf_op jit(solution)/shard_map/qy,xy->qx/dot_general | solution.py:31
  18.4 0.0 copy-done.3
  18.4 9.6 %fusion.33 = f32[512,128]{1,0:T(8,128)S(1)} fusion(s32[1024]{0:T(1024)S(1)} %iota_add_fusion, s32[512]{0:T(512)S(1)} %add_select_fusion.3, f32[2,128,1024]{2,1,0:T(8,128)S(1)} %copy-done.3), kind=kOutput, calls=%fused_computation.41 | convolution fusion | flops 813170688 | bytes 792576 | tf_op jit(solution)/shard_map/qy,xy->qx/dot_general | solution.py:31
  28.0 9.8 %fusion.49 = f32[512,1,128]{2,0,1:T(8,128)S(1)} fusion(f32[512,128]{1,0:T(8,128)S(1)} %fusion.32, s32[1024]{0:T(1024)S(1)} %iota_add_fusion, s32[512]{0:T(512)S(1)} %add_select_fusion.3, f32[2,128,1024]{2,1,0:T(8,128)S(1)} %copy-done.3), kind=kOutput, calls=%fused_computation.57 | convolution fusion | flops 813236224 | bytes 1054720 | tf_op jit(solution)/shard_map/qy,xy->qx/dot_general | solution.py:31
  37.8 0.0 copy-start.1
  37.8 9.6 %fusion.47 = f32[512,1,128]{2,0,1:T(8,128)S(1)} fusion(f32[512,128]{1,0:T(8,128)S(1)} %fusion.33, s32[1024]{0:T(1024)S(1)} %iota_add_fusion, s32[512]{0:T(512)S(1)} %add_select_fusion.3, f32[2,128,1024]{2,1,0:T(8,128)S(1)} %copy-done.3), kind=kOutput, calls=%fused_computation.55 | convolution fusion | flops 813236224 | bytes 1054720 | tf_op jit(solution)/shard_map/qy,xy->qx/dot_general | solution.py:31
  47.5 0.8 pad_maximum_fusion.2
  48.3 0.0 reduce-scatter.5.cloned.1.call-update
  48.3 0.0 all-reduce.3.cloned.1.call-start
  48.4 0.0 copy-done.1
  48.4 0.1 add_select_fusion.2
  48.5 75.2 %reduce-scatter.5.cloned.1.call-done = f32[32,2,128]{2,0,1:T(8,128)} async-done(((f32[512,2,128]{2,0,1:T(8,128)}), f32[32,2,128]{2,0,1:T(8,128)}) %reduce-scatter.5.cloned.1.call-update) | async-done | bytes 32784 | tf_op jit(solution)/shard_map/reduce_scatter | solution.py:50
  123.7 0.0 copy-start.4
  123.7 21.4 %fusion.5 = f32[16,512,32]{1,2,0:T(8,128)S(1)} fusion(s32[128]{0:T(128)S(1)} %iota_add_fusion.1, s32[16,512]{1,0:T(8,128)S(1)} %add_select_fusion.2, f32[32,2,128]{2,0,1:T(8,128)} %reduce-scatter.5.cloned.1.call-done), kind=kOutput, calls=%fused_computation.17 | convolution fusion | flops 418381824 | bytes 1098240 | tf_op jit(solution)/shard_map/qx,spx->sqp/dot_general | solution.py:31
  145.1 0.0 copy-done.4
  145.1 20.6 %fusion.6 = f32[16,512,32]{1,2,0:T(8,128)S(1)} fusion(s32[128]{0:T(128)S(1)} %iota_add_fusion.1, s32[16,512]{1,0:T(8,128)S(1)} %add_select_fusion.2, f32[32,2,128]{2,0,1:T(8,128)S(1)} %copy-done.4), kind=kOutput, calls=%fused_computation.18 | convolution fusion | flops 418381824 | bytes 1098240 | tf_op jit(solution)/shard_map/qx,spx->sqp/dot_general | solution.py:31
  165.7 20.8 %fusion.41 = f32[16,32,1,512]{3,1,0,2:T(8,128)S(1)} fusion(f32[16,512,32]{1,2,0:T(8,128)S(1)} %fusion.5, s32[128]{0:T(128)S(1)} %iota_add_fusion.1, s32[16,512]{1,0:T(8,128)S(1)} %add_select_fusion.2, f32[32,2,128]{2,0,1:T(8,128)S(1)} %copy-done.4), kind=kOutput, calls=%fused_computation.49 | convolution fusion | flops 418643968 | bytes 2146816 | tf_op jit(solution)/shard_map/qx,spx->sqp/dot_general | solution.py:31
  186.5 20.8 %fusion.39 = f32[16,32,1,512]{3,1,0,2:T(8,128)S(1)} fusion(f32[16,512,32]{1,2,0:T(8,128)S(1)} %fusion.6, s32[128]{0:T(128)S(1)} %iota_add_fusion.1, s32[16,512]{1,0:T(8,128)S(1)} %add_select_fusion.2, f32[32,2,128]{2,0,1:T(8,128)S(1)} %copy-done.4), kind=kOutput, calls=%fused_computation.47 | convolution fusion | flops 418643968 | bytes 2146816 | tf_op jit(solution)/shard_map/qx,spx->sqp/dot_general | solution.py:31
  207.3 1.5 pad_maximum_fusion
  208.8 0.0 copy-start.5
  208.8 0.0 copy-start
  208.8 0.0 copy-start.2
  208.8 0.0 all-reduce.3.cloned.1.call-update
  209.5 0.0 copy-done.5
  209.5 0.6 dynamic-slice
  210.1 0.0 copy-done
  210.1 0.0 copy-done.2
  210.1 0.2 convolution_add_fusion
  210.4 136.9 %all-reduce.3.cloned.1.call-done = f32[16,32,2,512]{3,1,0,2:T(8,128)} async-done(((f32[16,32,2,512]{3,1,0,2:T(8,128)}), f32[16,32,2,512]{3,1,0,2:T(8,128)}) %all-reduce.3.cloned.1.call-update) | async-done | bytes 2097168
  347.3 1.6 fusion.173
  348.8 1.6 stack.61
  350.4 4.9 all-to-all-start
  355.3 1.6 dynamic-slice_multiply_fusion
  356.8 0.8 copy.11
  357.6 36.3 %all-to-all-done = f32[16,1,32,2,512]{4,2,3,1,0:T(8,128)S(1)} async-done(((f32[16,1,32,2,512]{4,2,3,1,0:T(8,128)}), f32[16,1,32,2,512]{4,2,3,1,0:T(8,128)S(1)}, u32[]{:S(2)}, u32[]{:S(2)}) %all-to-all-start) | async-done | bytes 2097184 | tf_op jit(solution)/shard_map/all_to_all | solution.py:70
  393.9 0.2 copy.15
  394.1 19.3 %fusion.51 = f32[32,128]{1,0:T(8,128)S(1)} fusion(s32[128]{0:T(128)S(1)} %iota_add_fusion.1, s32[16,512]{1,0:T(8,128)S(1)} %add_select_fusion.2, f32[16,32,2,512]{3,1,0,2:T(8,128)S(1)} %bitcast.97), kind=kOutput, calls=%fused_computation.60 | convolution fusion | flops 418381824 | bytes 1098240 | tf_op jit(solution)/shard_map/mqp,mpx->qx/dot_general | solution.py:31
  413.4 19.3 %fusion.50 = f32[32,128]{1,0:T(8,128)S(1)} fusion(s32[128]{0:T(128)S(1)} %iota_add_fusion.1, s32[16,512]{1,0:T(8,128)S(1)} %add_select_fusion.2, f32[16,32,2,512]{3,1,0,2:T(8,128)S(1)} %bitcast.98), kind=kOutput, calls=%fused_computation.59 | convolution fusion | flops 418381824 | bytes 1098240 | tf_op jit(solution)/shard_map/mqp,mpx->qx/dot_general | solution.py:31
  432.7 19.2 %fusion.55 = f32[32,1,128]{2,0,1:T(8,128)S(1)} fusion(f32[32,128]{1,0:T(8,128)S(1)} %fusion.51, s32[128]{0:T(128)S(1)} %iota_add_fusion.1, s32[16,512]{1,0:T(8,128)S(1)} %add_select_fusion.2, f32[16,32,2,512]{3,1,0,2:T(8,128)S(1)} %bitcast.99), kind=kOutput, calls=%fused_computation.64 | convolution fusion | flops 418385920 | bytes 1114624 | tf_op jit(solution)/shard_map/mqp,mpx->qx/dot_general | solution.py:31
  451.8 19.2 %fusion.57 = f32[32,1,128]{2,0,1:T(8,128)S(1)} fusion(f32[32,128]{1,0:T(8,128)S(1)} %fusion.50, s32[128]{0:T(128)S(1)} %iota_add_fusion.1, s32[16,512]{1,0:T(8,128)S(1)} %add_select_fusion.2, f32[16,32,2,512]{3,1,0,2:T(8,128)S(1)} %bitcast.100), kind=kOutput, calls=%fused_computation.66 | convolution fusion | flops 418385920 | bytes 1114624 | tf_op jit(solution)/shard_map/mqp,mpx->qx/dot_general | solution.py:31
  471.0 38.3 %all_gather.3 = f32[512,2,128]{2,0,1:T(8,128)S(1)} all-gather(f32[32,2,128]{2,0,1:T(8,128)S(1)} %pad_maximum_fusion.3), channel_id=1, replica_groups=mesh['frow'=16,'fcol'=16] {'fcol'}, dimensions={0}, use_global_device_ids=true | all-gather | bytes 557056 | tf_op jit(solution)/shard_map/all_gather | solution.py:82
  509.4 9.0 %fusion.30 = f32[128,1024]{1,0:T(8,128)S(1)} fusion(s32[1024]{0:T(1024)S(1)} %iota_add_fusion, s32[512]{0:T(512)S(1)} %add_select_fusion.3, f32[512,2,128]{2,0,1:T(8,128)S(1)} %all_gather.3), kind=kOutput, calls=%fused_computation.38 | convolution fusion | flops 813170688 | bytes 792576 | tf_op jit(solution)/shard_map/qx,qy->xy/dot_general | solution.py:31
  518.4 9.4 %fusion.31 = f32[128,1024]{1,0:T(8,128)S(1)} fusion(s32[1024]{0:T(1024)S(1)} %iota_add_fusion, s32[512]{0:T(512)S(1)} %add_select_fusion.3, f32[512,2,128]{2,0,1:T(8,128)S(1)} %all_gather.3), kind=kOutput, calls=%fused_computation.39 | convolution fusion | flops 813170688 | bytes 792576 | tf_op jit(solution)/shard_map/qx,qy->xy/dot_general | solution.py:31
  527.8 9.2 %fusion.45 = f32[1,128,1024]{2,1,0:T(8,128)S(1)} fusion(f32[128,1024]{1,0:T(8,128)S(1)} %fusion.30, s32[1024]{0:T(1024)S(1)} %iota_add_fusion, s32[512]{0:T(512)S(1)} %add_select_fusion.3, f32[512,2,128]{2,0,1:T(8,128)S(1)} %all_gather.3), kind=kOutput, calls=%fused_computation.53 | convolution fusion | flops 813301760 | bytes 1316864 | tf_op jit(solution)/shard_map/qx,qy->xy/dot_general | solution.py:31
  537.0 9.1 %fusion.43 = f32[1,128,1024]{2,1,0:T(8,128)S(1)} fusion(f32[128,1024]{1,0:T(8,128)S(1)} %fusion.31, s32[1024]{0:T(1024)S(1)} %iota_add_fusion, s32[512]{0:T(512)S(1)} %add_select_fusion.3, f32[512,2,128]{2,0,1:T(8,128)S(1)} %all_gather.3), kind=kOutput, calls=%fused_computation.51 | convolution fusion | flops 813301760 | bytes 1316864 | tf_op jit(solution)/shard_map/qx,qy->xy/dot_general | solution.py:31
  546.1 1.1 pad_maximum_fusion.1
  (5 shorter events, 0.0 us)
Async XLA Ops:
  7.2 116.6 %reduce-scatter.5.cloned.1.call-start = ((), (), s32[]{:S(2)}) async-start(), calls=%async_computation.2 | async-start | bytes 557056 | tf_op jit(solution)/shard_map/reduce_scatter | solution.py:50
  7.9 10.5 %copy-start.3 = (f32[2,128,1024]{2,1,0:T(8,128)S(1)}, f32[2,128,1024]{2,1,0:T(8,128)}, u32[]{:S(2)}) copy-start(f32[2,128,1024]{2,1,0:T(8,128)} %param.6) | copy-start | bytes 3145732
  37.8 10.6 %copy-start.1 = (s32[16]{0:T(128)S(1)}, s32[16]{0:T(128)}, u32[]{:S(2)}) copy-start(s32[16]{0:T(128)} %param.8) | copy-start | bytes 196
  48.3 298.9 %all-reduce.3.cloned.1.call-start = ((), (), s32[]{:S(2)}) async-start(), calls=%async_computation.3 | async-start | bytes 4194304
  123.7 21.4 %copy-start.4 = (f32[32,2,128]{2,0,1:T(8,128)S(1)}, f32[32,2,128]{2,0,1:T(8,128)}, u32[]{:S(2)}) copy-start(f32[32,2,128]{2,0,1:T(8,128)} %reduce-scatter.5.cloned.1.call-done) | copy-start | bytes 98308
  208.8 0.7 copy-start.5
  208.8 1.3 copy-start
  208.8 1.3 copy-start.2
  350.4 43.5 %all-to-all-start = ((f32[16,1,32,2,512]{4,2,3,1,0:T(8,128)}), f32[16,1,32,2,512]{4,2,3,1,0:T(8,128)S(1)}, u32[]{:S(2)}, u32[]{:S(2)}) async-start(f32[16,1,32,2,512]{4,2,3,1,0:T(8,128)} %stack.61), calls=%async_computation.1 | async-start | bytes 4194304 | tf_op jit(solution)/shard_map/all_to_all | solution.py:70
Sparse Core Ops, SparseCore 0:
  48.5 75.2 reduce-scatter.4
  209.0 138.2 all-reduce.2
